TPU v7x, 32 devices: a whole 2x2x4 slice. The times are simulated.
32 devices in a mesh: field: 4 (over y, x), gz: 8 (over z, core).
Axes of the slice: x: 2, y: 2, z: 4, core: 2. Of those that a mesh axis runs over, the one named last changes fastest.
Arguments:
- fields: bfloat16 [2048, 2, 8, 16, 256], P('gz', None, 'field'), may hold values from -8 to 8
- shells: int32 [2048, 16, 256], P('gz'), may hold values from 0 to 255
- mubins: int32 [2048, 16, 256], P('gz'), may hold values from 0 to 7, as said below
Outputs:
- power: float32 [3, 8, 256], replicated
Inputs may be any that keep to these rules, and one draw needn't show every extreme that they name: `mubins`: A cell's mu-bin index is never above its k-shell index.
All inputs are finite; a program needn't handle non-finite values.
Results may differ from a plain program's by a relative error of at most 0.00052.
Values may be sent and summed in bfloat16 or wider, within the bound.
A program may use at most 192 MiB of HBM per device.

v0:
```python
import functools
import math

import jax
import jax.numpy as jnp
import numpy as np
from jax import lax
from jax.experimental import pallas as pl
from jax.experimental.pallas import tpu as pltpu
from jax.sharding import PartitionSpec as P

SHELLS = 256
MUBINS = 8
LANES = 128
LOW = 16
ROWS = 5
PAIRS = 8


def quarter_tables(length, zero):
    quarter, half = length // 4, length // 2
    unit = 2.0 * math.pi / length
    factor = 1.0 / math.sqrt(length)

    def pair(rows, stride):
        shape = (2, rows, half)
        parity = lax.broadcasted_iota(jnp.int32, shape, 0)
        row = lax.broadcasted_iota(jnp.int32, shape, 1) * stride + zero
        depth = 2 * lax.broadcasted_iota(jnp.int32, shape, 2) + parity
        angle = (row * depth % length).astype(jnp.float32) * unit
        return jnp.cos(angle), jnp.sin(angle)

    fine = 16
    ca, sa, cb, sb = lax.optimization_barrier(pair(quarter // fine, fine) + pair(fine, 1))
    ca, sa, cb, sb = ca[:, :, None], sa[:, :, None], cb[:, None], sb[:, None]
    cos_part = ((ca * cb - sa * sb) * factor).reshape(2, quarter, half)
    sin_part = ((sa * cb + ca * sb) * factor).reshape(2, quarter, half)
    row = lax.broadcasted_iota(jnp.int32, sin_part.shape, 1)
    column = lax.broadcasted_iota(jnp.int32, sin_part.shape, 2)
    alternate = (1 - 2 * (column % 2)).astype(jnp.float32) * factor
    sin_part = jnp.where(row == 0, alternate, sin_part)
    return jnp.concatenate(
        [cos_part.astype(jnp.bfloat16), sin_part.astype(jnp.bfloat16)], axis=1
    )


def round16(value):
    return value.astype(jnp.bfloat16).astype(jnp.float32)


def unpack(index_ref, keys):
    depth = index_ref.shape[1]

    def block(g, carry):
        word = index_ref[g]
        mu = word // 65536
        key = (word - mu * 65536) * MUBINS + mu
        upper = key // LOW
        rows = pl.ds(pl.multiple_of(g * depth, depth), depth)
        keys[0, rows, :] = (key - upper * LOW).astype(jnp.float32)
        keys[1, rows, :] = upper.astype(jnp.float32)
        return carry

    lax.fori_loop(0, index_ref.shape[0], block, 0)


def products(table_ref, lines_ref, prod, parity):
    half = table_ref.shape[1]

    def group(f, carry):
        right = lines_ref[f, :, parity].reshape(half, lines_ref.shape[-1])

        def rows_of(i, inner):
            rows = pl.ds(pl.multiple_of(i * 256, 256), 256)
            prod[f, parity, rows, :] = jnp.dot(
                table_ref[parity, rows, :], right, preferred_element_type=jnp.float32
            )
            return inner

        return lax.fori_loop(0, half // 256, rows_of, carry)

    lax.fori_loop(0, prod.shape[0], group, 0)


def local_kernel(length, table_ref, lines_ref, index_ref, wave_ref, out_ref, prod, vals, keys):
    unpack(index_ref, keys)
    products(table_ref, lines_ref, prod, 0)
    products(table_ref, lines_ref, prod, 1)
    bins(length, wave_ref, out_ref, prod, vals, keys)


def exchange_kernel(
    length, field_count, gz_count, table_ref, lines_ref, index_ref, wave_ref, out_ref,
    prod, vals, keys, lines, index, send, recv, own, index_send, index_recv, index_own,
):
    devices = field_count * gz_count
    me_field, me_gz = lax.axis_index("field"), lax.axis_index("gz")
    far = gz_count // 2
    mine = (gz_count - far) * field_count

    def peer(step):
        f = lax.rem(me_field + lax.rem(step, field_count), field_count)
        g = lax.rem(me_gz + step // field_count + far, gz_count)
        return f, g

    def others(run):
        def loop(step, carry):
            run(step)
            return carry

        lax.fori_loop(0, mine, loop, 0)
        lax.fori_loop(mine + 1, devices, loop, 0)

    def along(run):
        def loop(step, carry):
            run(step)
            return carry

        lax.fori_loop(1, gz_count, loop, 0)

    barrier = pltpu.get_barrier_semaphore()
    others(
        lambda step: pl.semaphore_signal(
            barrier, inc=1, device_id=peer(step), device_id_type=pl.DeviceIdType.MESH
        )
    )
    pl.semaphore_wait(barrier, devices - 1)

    def index_copy(step):
        g = lax.rem(me_gz + step, gz_count)
        return pltpu.make_async_remote_copy(
            src_ref=index_ref.at[g],
            dst_ref=index.at[me_gz],
            send_sem=index_send.at[step],
            recv_sem=index_recv.at[step],
            device_id=(me_field, g),
            device_id_type=pl.DeviceIdType.MESH,
        )

    def lines_copy(parity):
        def copy(step):
            f, g = peer(step)
            return pltpu.make_async_remote_copy(
                src_ref=lines_ref.at[f * gz_count + g, parity],
                dst_ref=lines.at[me_field, me_gz, parity],
                send_sem=send.at[parity, step],
                recv_sem=recv.at[parity, step],
                device_id=(f, g),
                device_id_type=pl.DeviceIdType.MESH,
            )

        return copy

    along(lambda step: index_copy(step).start())
    for parity in range(2):
        others(lambda step: lines_copy(parity)(step).start())
    me = me_field * gz_count + me_gz
    kept = [
        pltpu.make_async_copy(
            lines_ref.at[me, parity], lines.at[me_field, me_gz, parity], own.at[parity]
        )
        for parity in range(2)
    ]
    kept_index = pltpu.make_async_copy(index_ref.at[me_gz], index.at[me_gz], index_own)
    for copy in kept + [kept_index]:
        copy.start()

    kept_index.wait()
    along(lambda step: index_copy(step).wait_recv())
    unpack(index, keys)
    for parity in range(2):
        kept[parity].wait()
        others(lambda step: lines_copy(parity)(step).wait_recv())
        products(table_ref, lines, prod, parity)
    bins(length, wave_ref, out_ref, prod, vals, keys)
    along(lambda step: index_copy(step).wait_send())
    for parity in range(2):
        others(lambda step: lines_copy(parity)(step).wait_send())


def bins(length, wave_ref, out_ref, prod, vals, keys):
    quarter, half = length // 4, length // 2
    groups, local = prod.shape[0], prod.shape[3] // (2 * LANES)
    fields = groups * local
    out_ref[...] = jnp.zeros_like(out_ref)
    wave_x = wave_ref[0:1, :]
    wave_y = wave_ref[1:2, :]
    low_iota = lax.broadcasted_iota(jnp.int32, (16, LANES), 0).astype(jnp.float32)
    iotas = [(low_iota + 16.0 * j).astype(jnp.bfloat16) for j in range(LANES // 16)]
    one = jnp.ones((16, LANES), jnp.bfloat16)
    none = jnp.zeros((16, LANES), jnp.bfloat16)

    def cell_row(j, k):
        start = 1 - (k + quarter - 1) // quarter
        return (
            k,
            half - k,
            half + k - quarter * start,
            length - k - quarter * start,
        )[j]

    def tile(t, carry):
        first = pl.multiple_of(t * 8, 8)
        row = lax.broadcasted_iota(jnp.int32, (8, LANES), 0) + first
        special = row == 0

        def load(a, c, parity, sine):
            g, i = a // local, a % local
            at = (c * local + i) * LANES
            return prod[g, parity, pl.ds(sine * quarter + first, 8), at : at + LANES]

        def spectra(a):
            parts = []
            for c in range(2):
                ec, oc = load(a, c, 0, 0), load(a, c, 1, 0)
                es, os = load(a, c, 0, 1), load(a, c, 1, 1)
                p, q, m, n = ec + oc, es + os, ec - oc, os - es
                parts.append(
                    (
                        (p, jnp.where(special, 0.0, q)),
                        (m, jnp.where(special, 0.0, n)),
                        (jnp.where(special, es, m), jnp.where(special, os, -n)),
                        (jnp.where(special, es, p), jnp.where(special, -os, -q)),
                    )
                )
            u, v = parts
            return [(u[j][0] + v[j][1], v[j][0] - u[j][1]) for j in range(4)]

        k = row.astype(jnp.float32)
        zero_wave = (0.0, -half, quarter, -quarter)
        waves = (k, half - k, k - half, -k)
        base = spectra(0)
        second = None
        totals = [None] * 4
        saved = [None] * 4
        pending = [None] * 4
        for a in range(fields):
            spec = base if a == 0 else spectra(a)
            for j in range(4):
                cross = base[j][0] * spec[j][0] + base[j][1] * spec[j][1]
                if a == 0:
                    wz = jnp.where(special, float(zero_wave[j]), waves[j])
                    square = wave_x * wave_x + wave_y * wave_y + wz * wz
                    saved[j] = (wz, 1.0 / square)
                    vals[0, j * 8 : j * 8 + 8] = round16(cross)
                    continue
                wz, inverse = saved[j]
                if a == 1:
                    vals[1, j * 8 : j * 8 + 8] = round16(cross)
                    term = -0.5 * cross
                else:
                    weight = (
                        1.5 * wave_x * wave_x,
                        1.5 * wave_y * wave_y,
                        1.5 * wz * wz,
                        3.0 * wave_x * wave_y,
                        3.0 * wave_x * wz,
                        3.0 * wave_y * wz,
                    )[a - 2]
                    term = weight * inverse * cross
                pending[j] = term if pending[j] is None else pending[j] + term
                if a % local == local - 1:
                    rounded = round16(pending[j])
                    totals[j] = rounded if totals[j] is None else totals[j] + rounded
                    pending[j] = None
        for j in range(4):
            high = round16(totals[j])
            vals[2, j * 8 : j * 8 + 8] = high
            vals[3, j * 8 : j * 8 + 8] = totals[j] - high
        total = out_ref[...]
        for start in range(0, 32, PAIRS):
            left, hot = [], []
            for r in range(start, start + PAIRS):
                cell = cell_row(r // 8, first + r % 8)
                spread = [
                    jnp.broadcast_to(part, (16, LANES)).astype(jnp.bfloat16)
                    for part in [vals[i, r : r + 1] for i in range(4)]
                    + [keys[i, pl.ds(cell, 1), :] for i in range(2)]
                ]
                match = spread[4] == iotas[0]
                left.append(
                    jnp.concatenate(
                        [jnp.where(match, spread[i], none) for i in range(4)]
                        + [jnp.where(match, one, none)],
                        axis=0,
                    )
                )
                hot.append(
                    jnp.concatenate(
                        [jnp.where(spread[5] == it, one, none) for it in iotas], axis=0
                    )
                )
            total = total + lax.dot_general(
                jnp.concatenate(left, axis=1),
                jnp.concatenate(hot, axis=1),
                (((1,), (1,)), ((), ())),
                preferred_element_type=jnp.float32,
            )
        out_ref[...] = total
        return carry

    lax.fori_loop(0, quarter // 8, tile, 0)


def relayout_kernel(fields_ref, out_ref):
    for c in range(2):
        for i in range(fields_ref.shape[2]):
            at = (c * fields_ref.shape[2] + i) * LANES
            for h in range(out_ref.shape[1]):
                block = fields_ref[:, c, i, :, h * LANES : (h + 1) * LANES]
                block = block.reshape(16, 2, block.shape[1], LANES)
                for parity in range(2):
                    out_ref[:, h, parity, :, at : at + LANES] = jnp.swapaxes(
                        block[:, parity], 0, 1
                    )


def relayout(fields):
    depth, _, local, planes, yrows = fields.shape
    parts = yrows // LANES
    out = pl.pallas_call(
        relayout_kernel,
        grid=(depth // 32,),
        out_shape=jax.ShapeDtypeStruct(
            (planes, parts, 2, depth // 2, 2 * local * LANES), fields.dtype
        ),
        in_specs=[pl.BlockSpec((32, 2, local, planes, yrows), lambda i: (i, 0, 0, 0, 0))],
        out_specs=pl.BlockSpec(
            (planes, parts, 2, 16, 2 * local * LANES), lambda i: (0, 0, 0, i, 0)
        ),
    )(fields)
    return out.reshape(planes * parts, 2, depth // 2, 2 * local * LANES)


def reduce_kernel(field_count, gz_count, mine_ref, out_ref, parts, answer, send, recv, send2, recv2):
    devices = field_count * gz_count
    me_field, me_gz = lax.axis_index("field"), lax.axis_index("gz")
    me = me_field * gz_count + me_gz

    def peer(step):
        other = lax.rem(me + step, devices)
        return other, (other // gz_count, lax.rem(other, gz_count))

    barrier = pltpu.get_barrier_semaphore()

    def greet(step, carry):
        _, place = peer(step)
        pl.semaphore_signal(
            barrier, inc=1, device_id=place, device_id_type=pl.DeviceIdType.MESH
        )
        return carry

    lax.fori_loop(1, devices, greet, 0)
    pl.semaphore_wait(barrier, devices - 1)

    def scatter(step):
        other, place = peer(step)
        return pltpu.make_async_remote_copy(
            src_ref=mine_ref.at[other],
            dst_ref=parts.at[step],
            send_sem=send.at[step],
            recv_sem=recv.at[step],
            device_id=place,
            device_id_type=pl.DeviceIdType.MESH,
        )

    def gather(step):
        _, place = peer(step)
        return pltpu.make_async_remote_copy(
            src_ref=answer,
            dst_ref=out_ref.at[me],
            send_sem=send2.at[step],
            recv_sem=recv2.at[step],
            device_id=place,
            device_id_type=pl.DeviceIdType.MESH,
        )

    def start(copy):
        def run(step, carry):
            copy(step).start()
            return carry

        lax.fori_loop(1, devices, run, 0)

    start(scatter)

    def collect(step, total):
        scatter(step).wait_recv()
        return total + parts[step]

    answer[...] = lax.fori_loop(1, devices, collect, mine_ref[me])
    start(gather)
    out_ref[me] = answer[...]

    def finish(step, carry):
        scatter(step).wait_send()
        gather(step).wait()
        return carry

    lax.fori_loop(1, devices, finish, 0)


def all_reduce(total, field_count, gz_count):
    devices = field_count * gz_count
    rows = max(1, total.shape[0] // devices)
    total = jnp.pad(total, ((0, devices * rows - total.shape[0]), (0, 0)))
    total = total.reshape(devices, rows, LANES)
    return pl.pallas_call(
        functools.partial(reduce_kernel, field_count, gz_count),
        out_shape=jax.ShapeDtypeStruct(total.shape, jnp.float32),
        in_specs=[pl.BlockSpec(memory_space=pltpu.VMEM)],
        out_specs=pl.BlockSpec(memory_space=pltpu.VMEM),
        scratch_shapes=[
            pltpu.VMEM(total.shape, jnp.float32),
            pltpu.VMEM(total.shape[1:], jnp.float32),
            pltpu.SemaphoreType.DMA((devices,)),
            pltpu.SemaphoreType.DMA((devices,)),
            pltpu.SemaphoreType.DMA((devices,)),
            pltpu.SemaphoreType.DMA((devices,)),
        ],
        compiler_params=pltpu.CompilerParams(collective_id=0, has_side_effects=True),
    )(total).reshape(devices * rows, LANES)


def body(fields, shells, mubins):
    depth_local, _, local_fields, planes, yrows = fields.shape
    gz_count, field_count = lax.axis_size("gz"), lax.axis_size("field")
    devices = gz_count * field_count
    length = depth_local * gz_count
    half = length // 2
    plane_rows = planes * yrows
    width = plane_rows // devices
    me_gz, me_field = lax.axis_index("gz"), lax.axis_index("field")

    exchange = width == LANES and depth_local % 32 == 0
    if exchange:
        lines = relayout(fields)
    else:
        lines = fields.reshape(depth_local // 2, 2, 2, local_fields, devices, width)
        lines = lines.transpose(4, 1, 0, 2, 3, 5).reshape(
            devices, 2, depth_local // 2, 2 * local_fields * width
        )

    share = planes // field_count
    shells, mubins = (
        lax.dynamic_slice_in_dim(ids, me_field * share, share, 1) for ids in (shells, mubins)
    )
    index = (shells + mubins * 65536).reshape(depth_local, gz_count, width).transpose(1, 0, 2)

    span = 2 * local_fields * LANES
    table = quarter_tables(length, jnp.minimum(me_gz, 0))
    column = (me_field * gz_count + me_gz) * width + jnp.arange(LANES, dtype=jnp.int32)
    waves = jnp.stack([length // 4 + column // yrows, length // 8 + column % yrows])
    waves = jnp.pad(waves.astype(jnp.float32), ((0, 6), (0, 0)))
    landed = (field_count, gz_count, 2, depth_local // 2, span)
    scratch = [
        pltpu.VMEM((field_count, 2, half, span), jnp.float32),
        pltpu.VMEM((4, 32, LANES), jnp.float32),
        pltpu.VMEM((2, length, LANES), jnp.float32),
    ]
    vmem, anywhere = pl.BlockSpec(memory_space=pltpu.VMEM), pl.BlockSpec(memory_space=pl.ANY)
    if exchange:
        run, places, wide = (
            functools.partial(exchange_kernel, length, field_count, gz_count),
            anywhere,
            dict(collective_id=1, has_side_effects=True),
        )
        scratch += [
            pltpu.VMEM(landed, jnp.bfloat16),
            pltpu.VMEM((gz_count, depth_local, LANES), jnp.int32),
            pltpu.SemaphoreType.DMA((2, devices)),
            pltpu.SemaphoreType.DMA((2, devices)),
            pltpu.SemaphoreType.DMA((2,)),
            pltpu.SemaphoreType.DMA((gz_count,)),
            pltpu.SemaphoreType.DMA((gz_count,)),
            pltpu.SemaphoreType.DMA,
        ]
    else:
        run, places, wide = functools.partial(local_kernel, length), vmem, {}
        lines = lax.all_to_all(lines, ("field", "gz"), split_axis=0, concat_axis=0, tiled=True)
        lines = lines.reshape(landed[:-1] + (2 * local_fields, width))
        lines = jnp.pad(lines, ((0, 0),) * 5 + ((0, LANES - width),)).reshape(landed)
        index = lax.all_to_all(index, "gz", split_axis=0, concat_axis=0, tiled=True)
        index = jnp.pad(index, ((0, 0), (0, 0), (0, LANES - width)), constant_values=SHELLS)

    total = pl.pallas_call(
        run,
        out_shape=jax.ShapeDtypeStruct((ROWS * LOW, LANES), jnp.float32),
        in_specs=[vmem, places, places, vmem],
        out_specs=vmem,
        scratch_shapes=scratch,
        compiler_params=pltpu.CompilerParams(vmem_limit_bytes=56 * 1024 * 1024, **wide),
    )(table, lines, index, waves)

    total = total.reshape(ROWS, LOW, LANES)
    total = jnp.concatenate([total[:2], total[2:3] + total[3:4], total[4:]])
    total = all_reduce(total.reshape(-1, LANES), field_count, gz_count)[: 4 * LOW]
    total = total.reshape(4, 2, MUBINS, LANES).transpose(0, 2, 3, 1)
    total = total.reshape(4, MUBINS, SHELLS)
    return total[:3] / jnp.maximum(total[3], 1.0)[None]


def solution(mesh):
    in_specs = (P("gz", None, "field", None, None), P("gz", None, None), P("gz", None, None))
    return jax.shard_map(body, mesh=mesh, in_specs=in_specs, out_specs=P(), check_vma=False)
```

profile of v0, /device:TPU:0, one launch (start us, length us, event | category | flops | bytes accessed | tf_op | source)
XLA Modules:
  0.0 294.6 jit_solution(10308597897548692869)
XLA Ops:
  0.1 0.6 pad.4.wave_ref
  0.7 1.2 fusion.9
  1.9 1.8 fusion.4
  3.8 2.6 constant_dynamic-slice_fusion
  6.3 0.4 copy.11
  6.7 0.4 copy.10
  7.1 0.1 multiply_add_fusion
  7.3 0.0 copy-start
  7.3 0.0 copy-start.1
  7.3 1.4 copy.7
  8.7 1.9 add_multiply_fusion
  10.6 0.5 fusion
  11.1 0.0 copy-done
  11.1 0.0 copy-done.1
  11.1 0.8 multiply_convert_fusion
  11.9 2.4 pad_maximum_fusion.table_ref
  14.3 9.9 %shard_map.37 = bf16[16,2,2,128,512]{4,3,2,1,0:T(8,128)(2,1)} custom-call(bf16[256,2,2,16,256]{4,3,2,1,0:T(8,128)(2,1)} %fields_ref.1), custom_call_target="tpu_custom_call" | custom-call | tf_op jit(solution)/shard_map/pallas_call | solution.py:321
  24.2 250.5 %shard_map.38 = f32[80,128]{1,0:T(8,128)} custom-call(bf16[2,1024,1024]{2,1,0:T(8,128)(2,1)} %pad_maximum_fusion.table_ref, bf16[32,2,128,512]{3,2,1,0:T(8,128)(2,1)} %bitcast.18, s32[8,256,128]{2,1,0:T(8,128)} %bitcast.21, f32[8,128]{1,0:T(8,128)} %pad.4.wave_ref), custom_call_target="tpu_custom_call" | custom-call | tf_op jit(solution)/shard_map/pallas_call | solution.py:486
  274.7 0.7 slice.30
  275.5 0.7 add_bitcast_fusion
  276.2 0.6 pad_maximum_fusion.1
  276.8 15.9 %shard_map.39 = f32[32,2,128]{2,1,0:T(2,128)} custom-call(f32[32,2,128]{2,1,0:T(2,128)} %bitcast.27), custom_call_target="tpu_custom_call" | custom-call | tf_op jit(solution)/shard_map/pallas_call | solution.py:408
  292.7 1.0 copy.8
  293.7 0.1 slice_maximum_fusion
  293.8 0.7 copy.9
  (10 shorter events, 0.1 us)
Async XLA Ops:
  7.3 3.8 %copy-start = (f32[2,32,1024]{2,1,0:T(8,128)S(1)}, f32[2,32,1024]{2,1,0:T(8,128)}, u32[]{:S(2)}) copy-start(f32[2,32,1024]{2,1,0:T(8,128)} %get-tuple-element.9) | copy-start | bytes 786436
  7.3 3.8 %copy-start.1 = (f32[2,16,1024]{2,1,0:T(8,128)S(1)}, f32[2,16,1024]{2,1,0:T(8,128)}, u32[]{:S(2)}) copy-start(f32[2,16,1024]{2,1,0:T(8,128)} %get-tuple-element.10) | copy-start | bytes 393220
where the time goes:
time: 295 us
  Pallas kernels  276 us (94%)
  other arithmetic  10.3 us (3%)
  local copies, waits for them, and re-layouts  7.83 us (3%)
    pallas_call x1, Pallas kernels, body(): pl.pallas_call(run, out_shape=jax.ShapeDtypeStruct((ROWS * LOW, LANES), j...  251 us
    pallas_call x1, Pallas kernels, all_reduce(): pl.pallas_call(functools.partial(reduce_kernel, field_count, gz_count), o...  15.9 us
    pallas_call x1, Pallas kernels, relayout(): pl.pallas_call(relayout_kernel, grid=(depth // 32,), out_shape=jax.ShapeD...  9.87 us

commit v1 on v0

--- a/solution.py
+++ b/solution.py
@@ -422,6 +422,520 @@
     )(total).reshape(devices * rows, LANES)
 
 
+SLOTS = 6
+KEPT = 5
+
+
+def wave_tables(length):
+    quarter, half = length // 4, length // 2
+    unit = 2.0 * math.pi / length
+
+    def pair(rows, stride):
+        row = np.arange(rows)[None, :, None] * stride
+        depth = 2 * np.arange(half)[None, None, :] + np.arange(2)[:, None, None]
+        angle = (row * depth % length).astype(np.float32) * np.float32(unit)
+        return np.cos(angle), np.sin(angle)
+
+    ca, sa = pair(quarter // 16, 16)
+    cb, sb = pair(16, 1)
+    return np.stack([ca, sa]), np.stack([cb, sb])
+
+
+def build_table(length, coarse_ref, fine_ref, table):
+    quarter, half = length // 4, length // 2
+    factor = 1.0 / math.sqrt(length)
+    parts = table.shape[0]
+    wide = half // parts
+
+    def rows_of(a, carry):
+        rows = pl.ds(pl.multiple_of(a * 16, 16), 16)
+        under = pl.ds(pl.multiple_of(quarter + a * 16, 16), 16)
+        for parity in range(2):
+            for q in range(parts):
+                at = slice(q * wide, (q + 1) * wide)
+                ca, sa = (coarse_ref[i, parity, pl.ds(a, 1), at] for i in range(2))
+                cb, sb = (fine_ref[i, parity, :, at] for i in range(2))
+                cos_part = (ca * cb - sa * sb) * factor
+                sin_part = (sa * cb + ca * sb) * factor
+                row = lax.broadcasted_iota(jnp.int32, sin_part.shape, 0) + a
+                column = lax.broadcasted_iota(jnp.int32, sin_part.shape, 1)
+                alternate = (1 - 2 * (column % 2)).astype(jnp.float32) * factor
+                sin_part = jnp.where(row == 0, alternate, sin_part)
+                table[q, parity, rows, :] = cos_part.astype(jnp.bfloat16)
+                table[q, parity, under, :] = sin_part.astype(jnp.bfloat16)
+        return carry
+
+    lax.fori_loop(0, quarter // 16, rows_of, 0)
+
+
+def split_keys(index, keys):
+    depth = index.shape[1]
+
+    def block(g, carry):
+        word = index[g]
+        mu = lax.shift_right_logical(word, 16)
+        shell = word & 65535
+        rows = pl.ds(pl.multiple_of(g * depth, depth), depth)
+        keys[0, rows, :] = (mu + MUBINS * lax.shift_right_logical(shell, 7)).astype(jnp.float32)
+        keys[1, rows, :] = (shell & (LANES - 1)).astype(jnp.float32)
+        return carry
+
+    lax.fori_loop(0, index.shape[0], block, 0)
+
+
+def arrange(length, me_field, stage, spread, chunk):
+    planes = stage.shape[3]
+    rows = pl.ds(pl.multiple_of(chunk * 16, 16), 16)
+
+    def put(block, h, i, c):
+        block = block.reshape(16, 2, planes, LANES)
+        for parity in range(2):
+            spread[:, h, i, parity, rows, c * LANES : (c + 1) * LANES] = jnp.swapaxes(
+                block[:, parity], 0, 1
+            )
+
+    def take(c, i, h):
+        return stage[:, c, i, :, h * LANES : (h + 1) * LANES]
+
+    @pl.when(me_field % 2 == 0)
+    def _():
+        for c in range(2):
+            for i in range(2):
+                for h in range(2):
+                    put(take(c, i, h), h, i, c)
+
+    @pl.when(me_field % 2 == 1)
+    def _():
+        wave_x = lax.broadcasted_iota(jnp.int32, (planes, LANES), 0).astype(jnp.float32)
+        wave_x = wave_x + float(length // 4)
+        squared = me_field == 1
+        for h in range(2):
+            wave_y = lax.broadcasted_iota(jnp.int32, (planes, LANES), 1).astype(jnp.float32)
+            wave_y = wave_y + float(length // 8 + h * LANES)
+            first = jnp.where(squared, 1.5 * wave_x * wave_x, wave_x)[None]
+            other = jnp.where(squared, 1.5 * wave_y * wave_y, wave_y)[None]
+            for c in range(2):
+                value = first * take(c, 0, h).astype(jnp.float32)
+                value = value + other * take(c, 1, h).astype(jnp.float32)
+                put(value.astype(jnp.bfloat16), h, 0, c)
+
+
+def accumulate(table, land, prod, plane, fresh):
+    half = prod.shape[2]
+
+    def group(n, carry):
+        a, parity = n // 2, n % 2
+        right = land[plane, a, parity].reshape(-1, land.shape[-1])
+
+        def rows_of(r, inner):
+            rows = pl.ds(pl.multiple_of(r * 256, 256), 256)
+            part = jnp.dot(
+                table[plane, parity, rows, :], right, preferred_element_type=jnp.float32
+            )
+            prod[a, parity, rows, :] = part if fresh else prod[a, parity, rows, :] + part
+            return inner
+
+        return lax.fori_loop(0, half // 256, rows_of, carry)
+
+    lax.fori_loop(0, 2 * KEPT, group, 0)
+
+
+def histogram(length, plane, prod, vals, keys, acc):
+    quarter, half = length // 4, length // 2
+    acc[...] = jnp.zeros_like(acc)
+    lane = lax.broadcasted_iota(jnp.int32, (8, LANES), 1).astype(jnp.float32)
+    wave_x = (length // 4 + plane // 2).astype(jnp.float32)
+    wave_y = (length // 8 + (plane % 2) * LANES).astype(jnp.float32) + lane
+    flat = wave_x * wave_x + wave_y * wave_y
+    low_iota = lax.broadcasted_iota(jnp.int32, (16, LANES), 0).astype(jnp.float32)
+    iotas = [(low_iota + 16.0 * j).astype(jnp.bfloat16) for j in range(LANES // 16)]
+    one = jnp.ones((16, LANES), jnp.bfloat16)
+    none = jnp.zeros((16, LANES), jnp.bfloat16)
+
+    def cell_row(j, k):
+        start = 1 - (k + quarter - 1) // quarter
+        return (
+            k,
+            half - k,
+            half + k - quarter * start,
+            length - k - quarter * start,
+        )[j]
+
+    def tile(t, edge):
+        first = t * 8 if edge else pl.multiple_of(t * 8, 8)
+        row = lax.broadcasted_iota(jnp.int32, (8, LANES), 0) + first
+        special = row == 0
+
+        def load(a, c, parity, sine):
+            at = pl.ds(sine * quarter + first, 8)
+            return prod[a, parity, at, c * LANES : (c + 1) * LANES]
+
+        def spectra(a):
+            parts = []
+            for c in range(2):
+                ec, oc = load(a, c, 0, 0), load(a, c, 1, 0)
+                es, os = load(a, c, 0, 1), load(a, c, 1, 1)
+                p, q, m, n = ec + oc, es + os, ec - oc, os - es
+                if edge:
+                    parts.append(
+                        (
+                            (p, jnp.where(special, 0.0, q)),
+                            (m, jnp.where(special, 0.0, n)),
+                            (jnp.where(special, es, m), jnp.where(special, os, -n)),
+                            (jnp.where(special, es, p), jnp.where(special, -os, -q)),
+                        )
+                    )
+                else:
+                    parts.append(((p, q), (m, n), (m, n), (p, q)))
+            u, v = parts
+            result = []
+            for j in range(4):
+                if edge or j < 2:
+                    result.append((u[j][0] + v[j][1], v[j][0] - u[j][1]))
+                else:
+                    result.append((u[j][0] - v[j][1], v[j][0] + u[j][1]))
+            return result
+
+        k = row.astype(jnp.float32)
+        zero_wave = (0.0, -half, quarter, -quarter)
+        waves = [k, half - k, k - half, -k]
+        if edge:
+            waves = [jnp.where(special, float(z), w) for z, w in zip(zero_wave, waves)]
+            inverse = [1.0 / (flat + w * w) for w in waves]
+        else:
+            inverse = [1.0 / (flat + w * w) for w in waves[:2]]
+            inverse = [inverse[0], inverse[1], inverse[1], inverse[0]]
+        cross_b, base, first_cross, cubic, mixed = (spectra(a) for a in range(KEPT))
+        for j in range(4):
+            re, im = base[j]
+            auto = re * re + im * im
+            pair = re * first_cross[j][0] + im * first_cross[j][1]
+            w = waves[j]
+            three, half_more = 3.0 * w, 1.5 * (w * w)
+            qre = mixed[j][0] + three * cross_b[j][0] + half_more * cubic[j][0]
+            qim = mixed[j][1] + three * cross_b[j][1] + half_more * cubic[j][1]
+            quad = inverse[j] * (re * qre + im * qim) - 0.5 * pair
+            vals[0, j * 8 : j * 8 + 8] = auto
+            vals[1, j * 8 : j * 8 + 8] = pair
+            vals[2, j * 8 : j * 8 + 8] = quad
+        total = acc[...]
+        for start in range(0, 32, PAIRS):
+            left, hot = [], []
+            for r in range(start, start + PAIRS):
+                cell = cell_row(r // 8, first + r % 8)
+                spread = [
+                    jnp.broadcast_to(part, (16, LANES)).astype(jnp.bfloat16)
+                    for part in [vals[i, r : r + 1] for i in range(3)]
+                    + [keys[i, pl.ds(cell, 1), :] for i in range(2)]
+                ]
+                match = spread[3] == iotas[0]
+                left.append(
+                    jnp.concatenate(
+                        [jnp.where(match, spread[i], none) for i in range(3)]
+                        + [jnp.where(match, one, none)],
+                        axis=0,
+                    )
+                )
+                hot.append(
+                    jnp.concatenate(
+                        [jnp.where(spread[4] == it, one, none) for it in iotas], axis=0
+                    )
+                )
+            total = total + lax.dot_general(
+                jnp.concatenate(left, axis=1),
+                jnp.concatenate(hot, axis=1),
+                (((1,), (1,)), ((), ())),
+                preferred_element_type=jnp.float32,
+            )
+        acc[...] = total
+
+    tile(0, True)
+
+    def step(t, carry):
+        tile(t, False)
+        return carry
+
+    lax.fori_loop(1, quarter // 8, step, 0)
+
+
+def whole_kernel(
+    length, coarse_ref, fine_ref, fields_ref, shells_ref, mubins_ref, out_ref,
+    stage, spread, mix, joined, land, prod, table, raw, index_out, index, keys, vals, acc,
+    parts, answer,
+    stage_sem, raw_sem, index_sent, index_come, mix_sent, mix_come, land_sent, land_come,
+    part_sent, part_come, answer_sent, answer_come,
+):
+    fields, cores = 4, 2
+    planes_z = land.shape[0]
+    gz_count = planes_z * cores
+    devices = fields * gz_count
+    me_field, me_gz = lax.axis_index("field"), lax.axis_index("gz")
+    me = me_field * gz_count + me_gz
+    me_plane, me_core = me_gz // cores, me_gz % cores
+    chunks = fields_ref.shape[0] // 32
+    MESH = pl.DeviceIdType.MESH
+
+    def loop(low, high, run):
+        def step(i, carry):
+            run(i)
+            return carry
+
+        lax.fori_loop(low, high, step, 0)
+
+    barrier = pltpu.get_barrier_semaphore()
+
+    def greet(step):
+        other = lax.rem(me + step, devices)
+        pl.semaphore_signal(
+            barrier, inc=1, device_id=(other // gz_count, lax.rem(other, gz_count)),
+            device_id_type=MESH,
+        )
+
+    loop(1, devices, greet)
+
+    def raw_copy(n):
+        b = n % gz_count
+        lanes = pl.ds(pl.multiple_of((b % 2) * LANES, LANES), LANES)
+        at = (slice(None), me_field * (gz_count // 2) + b // 2, lanes)
+        return [
+            pltpu.make_async_copy(ref.at[at], raw.at[i, b], raw_sem.at[i])
+            for i, ref in enumerate((shells_ref, mubins_ref))
+        ]
+
+    def fetch(n):
+        return pltpu.make_async_copy(
+            fields_ref.at[pl.ds(n * 32, 32)], stage.at[n % 2], stage_sem.at[n % 2]
+        )
+
+    loop(0, gz_count, lambda n: [copy.start() for copy in raw_copy(n)])
+    for n in range(2):
+        fetch(n).start()
+
+    def target(i):
+        plane = lax.rem(me_plane + 2 + i // 2, planes_z)
+        return plane * cores + lax.rem(me_core + i, cores)
+
+    for i in range(2):
+        pltpu.make_async_copy(raw.at[i], raw.at[i], raw_sem.at[i]).wait()
+
+    def join(n):
+        index_out[n] = raw[0, n] + raw[1, n] * 65536
+
+    loop(0, gz_count, join)
+    pl.semaphore_wait(barrier, devices - 1)
+
+    def index_send(i):
+        g = target(i)
+
+        @pl.when(g != me_gz)
+        def _():
+            pltpu.make_async_remote_copy(
+                src_ref=index_out.at[g], dst_ref=index.at[me_gz],
+                send_sem=index_sent, recv_sem=index_come,
+                device_id=(me_field, g), device_id_type=MESH,
+            ).start()
+
+        @pl.when(g == me_gz)
+        def _():
+            pltpu.make_async_copy(index_out.at[g], index.at[g], index_come).start()
+
+    loop(0, gz_count, index_send)
+
+    def place(n):
+        fetch(n).wait()
+        arrange(length, me_field, stage.at[n % 2], spread, n)
+
+        @pl.when(n + 2 < chunks)
+        def _():
+            fetch(n + 2).start()
+
+    loop(0, chunks, place)
+
+    even = 1 - me_field % 2
+    slot = even * (me_field + 1) + (1 - even) * ((15 - 5 * me_field) // 2)
+
+    def mix_send(i):
+        g = target(i)
+
+        def piece(f, s):
+            return spread.at[f * (gz_count // 2) + g // 2, g % 2, s]
+
+        def send(f, s):
+            pltpu.make_async_remote_copy(
+                src_ref=piece(f, s), dst_ref=mix.at[g, slot + s],
+                send_sem=mix_sent, recv_sem=mix_come.at[g],
+                device_id=(f, me_gz), device_id_type=MESH,
+            ).start()
+
+        def keep(s):
+            pltpu.make_async_copy(
+                piece(me_field, s), mix.at[g, slot + s], mix_come.at[g]
+            ).start()
+
+        others = [lax.rem(me_field + 2, 4), me_field + 1 - 2 * (me_field % 2), 3 - me_field]
+        for f in others:
+            send(f, 0)
+        keep(0)
+
+        @pl.when(even == 1)
+        def _():
+            for f in others:
+                send(f, 1)
+            keep(1)
+
+    loop(0, gz_count, mix_send)
+    build_table(length, coarse_ref, fine_ref, table)
+
+    def join_send(i):
+        g = target(i)
+        pltpu.make_async_copy(mix.at[g], mix.at[g], mix_come.at[g]).wait()
+        wave_x = (length // 4 + me_field * (gz_count // 2) + g // 2).astype(jnp.float32)
+        lane = lax.broadcasted_iota(jnp.int32, (1, 2 * LANES), 1) % LANES
+        wave_y = (length // 8 + (g % 2) * LANES + lane).astype(jnp.float32)
+        weight = 3.0 * wave_x * wave_y
+        for parity in range(2):
+            value = mix[g, 5, parity].astype(jnp.float32)
+            value = value + weight * mix[g, 4, parity].astype(jnp.float32)
+            joined[g, parity] = value.astype(jnp.bfloat16)
+        pairs = (
+            (mix.at[g, pl.ds(0, 4)], land.at[me_plane, pl.ds(0, 4), :, me_core]),
+            (joined.at[g], land.at[me_plane, 4, :, me_core]),
+        )
+
+        @pl.when(g != me_gz)
+        def _():
+            for source, goal in pairs:
+                pltpu.make_async_remote_copy(
+                    src_ref=source, dst_ref=goal,
+                    send_sem=land_sent, recv_sem=land_come.at[me_gz],
+                    device_id=(me_field, g), device_id_type=MESH,
+                ).start()
+
+        @pl.when(g == me_gz)
+        def _():
+            for source, goal in pairs:
+                pltpu.make_async_copy(source, goal, land_come.at[me_gz]).start()
+
+    loop(0, gz_count // 2, join_send)
+    pltpu.make_async_copy(index, index, index_come).wait()
+    split_keys(index, keys)
+    loop(gz_count // 2, gz_count, join_send)
+
+    for j in range(planes_z):
+        plane = lax.rem(me_plane + planes_z + 2 - j, planes_z)
+        for core in range(cores):
+            block = land.at[plane, :, :, core]
+            pltpu.make_async_copy(block, block, land_come.at[plane * cores + core]).wait()
+        accumulate(table, land, prod, plane, j == 0)
+
+    histogram(length, me_field * gz_count + me_gz, prod, vals, keys, acc)
+
+    ranks = acc.shape[0] // 8
+    root = lax.rem(me_gz, fields) == me_field
+
+    def part_copy(r):
+        return pltpu.make_async_remote_copy(
+            src_ref=acc.at[pl.ds(pl.multiple_of(r * 8, 8), 8)], dst_ref=parts.at[me],
+            send_sem=part_sent, recv_sem=part_come,
+            device_id=(lax.rem(r, fields), r), device_id_type=MESH,
+        )
+
+    def part_send(n):
+        r = lax.rem(me_gz + n, ranks)
+
+        @pl.when((r != me_gz) | jnp.logical_not(root))
+        def _():
+            part_copy(r).start()
+
+    loop(0, ranks, part_send)
+
+    def answer_copy(step):
+        other = lax.rem(me + step, devices)
+        return pltpu.make_async_remote_copy(
+            src_ref=answer.at[me_gz], dst_ref=answer.at[me_gz],
+            send_sem=answer_sent, recv_sem=answer_come,
+            device_id=(other // gz_count, lax.rem(other, gz_count)), device_id_type=MESH,
+        )
+
+    @pl.when(root)
+    def _():
+        parts[me] = acc[pl.ds(pl.multiple_of(me_gz * 8, 8), 8), :]
+        rest = parts.at[pl.ds(0, devices - 1)]
+        pltpu.make_async_copy(rest, rest, part_come).wait()
+        answer[me_gz] = lax.fori_loop(
+            1, devices, lambda d, total: total + parts[d], parts[0]
+        )
+        loop(1, devices, lambda step: answer_copy(step).start())
+        got = answer.at[pl.ds(0, ranks - 1)]
+        pltpu.make_async_copy(got, got, answer_come).wait()
+        pltpu.make_async_copy(rest, rest, answer_sent).wait()
+        pltpu.make_async_copy(got, got, part_sent).wait()
+
+    @pl.when(jnp.logical_not(root))
+    def _():
+        pltpu.make_async_copy(answer, answer, answer_come).wait()
+        pltpu.make_async_copy(answer, answer, part_sent).wait()
+
+    for hi in range(2):
+        scale = 1.0 / jnp.maximum(answer[6 + hi], 1.0)
+        for m in range(3):
+            out_ref[m, :, hi * LANES : (hi + 1) * LANES] = answer[2 * m + hi] * scale
+
+    sent = index_out.at[pl.ds(0, gz_count - 1)]
+    pltpu.make_async_copy(sent, sent, index_sent).wait()
+    sent = mix.at[pl.ds(0, gz_count - 1), pl.ds(0, KEPT)]
+    pltpu.make_async_copy(sent, sent, land_sent).wait()
+
+    @pl.when(even == 1)
+    def _():
+        sent = spread.at[pl.ds(0, 12)]
+        pltpu.make_async_copy(sent, sent, mix_sent).wait()
+
+    @pl.when(even == 0)
+    def _():
+        sent = spread.at[pl.ds(0, 12), :, 0]
+        pltpu.make_async_copy(sent, sent, mix_sent).wait()
+
+
+def whole(fields, shells, mubins, gz_count):
+    depth, _, local, planes, yrows = fields.shape
+    length = depth * gz_count
+    half = length // 2
+    coarse, fine = wave_tables(length)
+    vmem, anywhere = pl.BlockSpec(memory_space=pltpu.VMEM), pl.BlockSpec(memory_space=pl.ANY)
+    wide = 2 * LANES
+    dma = pltpu.SemaphoreType.DMA
+    low = jnp.bfloat16
+    return pl.pallas_call(
+        functools.partial(whole_kernel, length),
+        out_shape=jax.ShapeDtypeStruct((3, MUBINS, SHELLS), jnp.float32),
+        in_specs=[vmem, vmem, anywhere, anywhere, anywhere],
+        out_specs=vmem,
+        scratch_shapes=[
+            pltpu.VMEM((2, 32) + fields.shape[1:], low),
+            pltpu.VMEM((planes, 2, local, 2, depth // 2, wide), low),
+            pltpu.VMEM((gz_count, SLOTS, 2, depth // 2, wide), low),
+            pltpu.VMEM((gz_count, 2, depth // 2, wide), low),
+            pltpu.VMEM((gz_count // 2, KEPT, 2, 2, depth // 2, wide), low),
+            pltpu.VMEM((KEPT, 2, half, wide), jnp.float32),
+            pltpu.VMEM((gz_count // 2, 2, half, depth), low),
+            pltpu.VMEM((2, gz_count, depth, LANES), jnp.int32),
+            pltpu.VMEM((gz_count, depth, LANES), jnp.int32),
+            pltpu.VMEM((gz_count, depth, LANES), jnp.int32),
+            pltpu.VMEM((2, length, LANES), jnp.float32),
+            pltpu.VMEM((3, 32, LANES), jnp.float32),
+            pltpu.VMEM((4 * LOW, LANES), jnp.float32),
+            pltpu.VMEM((4 * gz_count, 8, LANES), jnp.float32),
+            pltpu.VMEM((8, 8, LANES), jnp.float32),
+            dma((2,)), dma((2,)), dma, dma, dma, dma((gz_count,)), dma, dma((gz_count,)),
+            dma, dma, dma, dma,
+        ],
+        compiler_params=pltpu.CompilerParams(
+            vmem_limit_bytes=60 * 1024 * 1024, collective_id=2, has_side_effects=True
+        ),
+    )(jnp.asarray(coarse), jnp.asarray(fine), fields, shells, mubins)
+
+
 def body(fields, shells, mubins):
     depth_local, _, local_fields, planes, yrows = fields.shape
     gz_count, field_count = lax.axis_size("gz"), lax.axis_size("field")
@@ -431,6 +945,10 @@
     plane_rows = planes * yrows
     width = plane_rows // devices
     me_gz, me_field = lax.axis_index("gz"), lax.axis_index("field")
+
+    if (field_count, gz_count, local_fields, planes, yrows) == (4, 8, 2, 16, 256):
+        if depth_local == 256 and (SHELLS, MUBINS) == (256, 8):
+            return whole(fields, shells, mubins, gz_count)
 
     exchange = width == LANES and depth_local % 32 == 0
     if exchange:

time: 295 us -> 205 us (0.69)
  Pallas kernels: 276 us -> 203 us
  other arithmetic: 10.3 us -> 0 us
  local copies, waits for them, and re-layouts: 7.83 us -> 1.35 us
    pallas_call x3 -> x1, Pallas kernels: 276 us -> 203 us  [whole(): pl.pallas_call(functools.partial(whole_kernel, length), out_shape=jax.Sha...]
    sin x2 -> x0, other arithmetic: 3.09 us -> none  [pair(): return (jnp.cos(angle), jnp.sin(angle))]
    concatenate x2 -> x0, other arithmetic: 3.01 us -> none  [the longest x1 2.4 us: quarter_tables(): jnp.concatenate([cos_part.astype(jnp.bfloat16), sin_part.astype(jnp.bfloa...]
where the time goes in v1:
time: 205 us
  Pallas kernels  203 us (99%)
    pallas_call x1, Pallas kernels, whole(): pl.pallas_call(functools.partial(whole_kernel, length), out_shape=jax.Sha...  203 us

profile of v1, /device:TPU:0, one launch (start us, length us, event | category | flops | bytes accessed | tf_op | source)
XLA Modules:
  0.0 204.8 jit_solution(9051171918575785780)
XLA Ops:
  0.0 203.5 %shard_map.55 = f32[3,8,256]{2,1,0:T(8,128)} custom-call(f32[2,2,32,1024]{3,2,1,0:T(8,128)} %constant.4.clone.coarse_ref, f32[2,2,16,1024]{3,2,1,0:T(8,128)} %constant.5.clone.fine_ref, bf16[256,2,2,16,256]{4,3,2,1,0:T(8,128)(2,1)} %fields_ref.1, s32[256,16,256]{2,1,0:T(8,128)} %shells_ref.1, s32[256,16,256]{2,1,0:T(8,128)} %mubins_ref.1), custom_call_target="tpu_custom_call" | custom-call | tf_op jit(solution)/shard_map/pallas_call | solution.py:909
  203.5 1.3 copy.7

commit v2 on v1

--- a/solution.py
+++ b/solution.py
@@ -521,21 +521,13 @@
 
 
 def accumulate(table, land, prod, plane, fresh):
-    half = prod.shape[2]
-
     def group(n, carry):
         a, parity = n // 2, n % 2
         right = land[plane, a, parity].reshape(-1, land.shape[-1])
 
-        def rows_of(r, inner):
-            rows = pl.ds(pl.multiple_of(r * 256, 256), 256)
-            part = jnp.dot(
-                table[plane, parity, rows, :], right, preferred_element_type=jnp.float32
-            )
-            prod[a, parity, rows, :] = part if fresh else prod[a, parity, rows, :] + part
-            return inner
-
-        return lax.fori_loop(0, half // 256, rows_of, carry)
+        part = jnp.dot(table[plane, parity], right, preferred_element_type=jnp.float32)
+        prod[a, parity] = part if fresh else prod[a, parity] + part
+        return carry
 
     lax.fori_loop(0, 2 * KEPT, group, 0)
 
@@ -711,8 +703,12 @@
     for n in range(2):
         fetch(n).start()
 
+    side = 1 + 2 * (me_plane // 2)
+
     def target(i):
-        plane = lax.rem(me_plane + 2 + i // 2, planes_z)
+        turn = i // 2
+        steps = (2 + 11 * turn * (turn - 1) // 2 - turn) * side
+        plane = lax.rem(me_plane + steps, planes_z)
         return plane * cores + lax.rem(me_core + i, cores)
 
     for i in range(2):
@@ -821,8 +817,9 @@
     split_keys(index, keys)
     loop(gz_count // 2, gz_count, join_send)
 
-    for j in range(planes_z):
-        plane = lax.rem(me_plane + planes_z + 2 - j, planes_z)
+    near = 1 - 2 * (me_plane % 2)
+    for j, steps in enumerate((2, near, 0, 2 + near)):
+        plane = lax.rem(me_plane + steps, planes_z)
         for core in range(cores):
             block = land.at[plane, :, :, core]
             pltpu.make_async_copy(block, block, land_come.at[plane * cores + core]).wait()

time: 205 us -> 192 us (0.937)
  Pallas kernels: 203 us -> 190 us
    pallas_call x1, Pallas kernels: 203 us -> 190 us  [whole(): pl.pallas_call(functools.partial(whole_kernel, length), out_shape=jax.Sha...]
where the time goes in v2:
time: 192 us
  Pallas kernels  190 us (99%)
    pallas_call x1, Pallas kernels, whole(): pl.pallas_call(functools.partial(whole_kernel, length), out_shape=jax.Sha...  190 us

profile of v2, /device:TPU:0, one launch (start us, length us, event | category | flops | bytes accessed | tf_op | source)
XLA Modules:
  0.0 191.5 jit_solution(17521982794162213873)
XLA Ops:
  0.0 190.2 %shard_map.55 = f32[3,8,256]{2,1,0:T(8,128)} custom-call(f32[2,2,32,1024]{3,2,1,0:T(8,128)} %constant.4.clone.coarse_ref, f32[2,2,16,1024]{3,2,1,0:T(8,128)} %constant.5.clone.fine_ref, bf16[256,2,2,16,256]{4,3,2,1,0:T(8,128)(2,1)} %fields_ref.1, s32[256,16,256]{2,1,0:T(8,128)} %shells_ref.1, s32[256,16,256]{2,1,0:T(8,128)} %mubins_ref.1), custom_call_target="tpu_custom_call" | custom-call | tf_op jit(solution)/shard_map/pallas_call | solution.py:906
  190.2 1.3 copy.7

commit v3 on v2

--- a/solution.py
+++ b/solution.py
@@ -520,21 +520,19 @@
                 put(value.astype(jnp.bfloat16), h, 0, c)
 
 
-def accumulate(table, land, prod, plane, fresh):
+def accumulate(table, land, prod, plane, local, fields, start, fresh):
     def group(n, carry):
         a, parity = n // 2, n % 2
-        right = land[plane, a, parity].reshape(-1, land.shape[-1])
-
+        right = land[local, a, parity].reshape(-1, land.shape[-1])
         part = jnp.dot(table[plane, parity], right, preferred_element_type=jnp.float32)
-        prod[a, parity] = part if fresh else prod[a, parity] + part
+        prod[start + a, parity] = part if fresh else prod[start + a, parity] + part
         return carry
 
-    lax.fori_loop(0, 2 * KEPT, group, 0)
-
-
-def histogram(length, plane, prod, vals, keys, acc):
+    lax.fori_loop(0, 2 * fields, group, 0)
+
+
+def histogram(length, plane, prod, vals, keys, acc, low, high):
     quarter, half = length // 4, length // 2
-    acc[...] = jnp.zeros_like(acc)
     lane = lax.broadcasted_iota(jnp.int32, (8, LANES), 1).astype(jnp.float32)
     wave_x = (length // 4 + plane // 2).astype(jnp.float32)
     wave_y = (length // 8 + (plane % 2) * LANES).astype(jnp.float32) + lane
@@ -597,7 +595,7 @@
         else:
             inverse = [1.0 / (flat + w * w) for w in waves[:2]]
             inverse = [inverse[0], inverse[1], inverse[1], inverse[0]]
-        cross_b, base, first_cross, cubic, mixed = (spectra(a) for a in range(KEPT))
+        base, first_cross, cross_b, cubic, mixed = (spectra(a) for a in range(KEPT))
         for j in range(4):
             re, im = base[j]
             auto = re * re + im * im
@@ -641,30 +639,34 @@
             )
         acc[...] = total
 
-    tile(0, True)
+    @pl.when(low == 0)
+    def _():
+        tile(0, True)
 
     def step(t, carry):
         tile(t, False)
         return carry
 
-    lax.fori_loop(1, quarter // 8, step, 0)
+    lax.fori_loop(jnp.maximum(low, 1), high, step, 0)
 
 
 def whole_kernel(
     length, coarse_ref, fine_ref, fields_ref, shells_ref, mubins_ref, out_ref,
-    stage, spread, mix, joined, land, prod, table, raw, index_out, index, keys, vals, acc,
+    stage, spread, mix, joined, first, land, prod, table, raw, index_out, index, keys, vals, acc,
     parts, answer,
-    stage_sem, raw_sem, index_sent, index_come, mix_sent, mix_come, land_sent, land_come,
-    part_sent, part_come, answer_sent, answer_come,
+    stage_sem, raw_sem, index_sent, index_come, mix_sent, mix_come, land_sent, first_come,
+    land_come, part_sent, part_come, answer_sent, answer_come,
 ):
-    fields, cores = 4, 2
-    planes_z = land.shape[0]
+    fields, cores, chunks = 4, 2, 2
+    planes_z = table.shape[0]
     gz_count = planes_z * cores
+    owners = gz_count // chunks
     devices = fields * gz_count
     me_field, me_gz = lax.axis_index("field"), lax.axis_index("gz")
     me = me_field * gz_count + me_gz
     me_plane, me_core = me_gz // cores, me_gz % cores
-    chunks = fields_ref.shape[0] // 32
+    me_half, me_owner = me_gz // owners, me_gz % owners
+    steps = fields_ref.shape[0] // 32
     MESH = pl.DeviceIdType.MESH
 
     def loop(low, high, run):
@@ -673,6 +675,9 @@
             return carry
 
         lax.fori_loop(low, high, step, 0)
+
+    def wait(ref, sem):
+        pltpu.make_async_copy(ref, ref, sem).wait()
 
     barrier = pltpu.get_barrier_semaphore()
 
@@ -685,8 +690,7 @@
 
     loop(1, devices, greet)
 
-    def raw_copy(n):
-        b = n % gz_count
+    def raw_copy(b):
         lanes = pl.ds(pl.multiple_of((b % 2) * LANES, LANES), LANES)
         at = (slice(None), me_field * (gz_count // 2) + b // 2, lanes)
         return [
@@ -699,20 +703,11 @@
             fields_ref.at[pl.ds(n * 32, 32)], stage.at[n % 2], stage_sem.at[n % 2]
         )
 
-    loop(0, gz_count, lambda n: [copy.start() for copy in raw_copy(n)])
+    loop(0, gz_count, lambda b: [copy.start() for copy in raw_copy(b)])
     for n in range(2):
         fetch(n).start()
-
-    side = 1 + 2 * (me_plane // 2)
-
-    def target(i):
-        turn = i // 2
-        steps = (2 + 11 * turn * (turn - 1) // 2 - turn) * side
-        plane = lax.rem(me_plane + steps, planes_z)
-        return plane * cores + lax.rem(me_core + i, cores)
-
     for i in range(2):
-        pltpu.make_async_copy(raw.at[i], raw.at[i], raw_sem.at[i]).wait()
+        wait(raw.at[i], raw_sem.at[i])
 
     def join(n):
         index_out[n] = raw[0, n] + raw[1, n] * 65536
@@ -720,20 +715,35 @@
     loop(0, gz_count, join)
     pl.semaphore_wait(barrier, devices - 1)
 
+    def owner_of(i):
+        plane = lax.rem(me_plane + 1 + (i % owners) // 2, 2)
+        return plane * cores + lax.rem(me_core + i, cores)
+
+    def forward(source, goal, sent, come, g):
+        pltpu.make_async_remote_copy(
+            src_ref=source, dst_ref=goal, send_sem=sent, recv_sem=come,
+            device_id=(me_field, g), device_id_type=MESH,
+        ).start()
+
     def index_send(i):
-        g = target(i)
-
-        @pl.when(g != me_gz)
+        chunk, owner = i // owners, owner_of(i)
+        b = chunk * owners + owner
+        goal = index.at[chunk, me_gz]
+        forward(
+            index_out.at[b], goal, index_sent, index_come.at[chunk],
+            (1 - me_half) * owners + owner,
+        )
+
+        @pl.when(owner != me_owner)
         def _():
-            pltpu.make_async_remote_copy(
-                src_ref=index_out.at[g], dst_ref=index.at[me_gz],
-                send_sem=index_sent, recv_sem=index_come,
-                device_id=(me_field, g), device_id_type=MESH,
-            ).start()
-
-        @pl.when(g == me_gz)
+            forward(
+                index_out.at[b], goal, index_sent, index_come.at[chunk],
+                me_half * owners + owner,
+            )
+
+        @pl.when(owner == me_owner)
         def _():
-            pltpu.make_async_copy(index_out.at[g], index.at[g], index_come).start()
+            pltpu.make_async_copy(index_out.at[b], goal, index_come.at[chunk]).start()
 
     loop(0, gz_count, index_send)
 
@@ -741,31 +751,31 @@
         fetch(n).wait()
         arrange(length, me_field, stage.at[n % 2], spread, n)
 
-        @pl.when(n + 2 < chunks)
+        @pl.when(n + 2 < steps)
         def _():
             fetch(n + 2).start()
 
-    loop(0, chunks, place)
+    loop(0, steps, place)
 
     even = 1 - me_field % 2
-    slot = even * (me_field + 1) + (1 - even) * ((15 - 5 * me_field) // 2)
+    slot = even * (3 * me_field // 2) + (1 - even) * ((13 - 3 * me_field) // 2)
 
     def mix_send(i):
-        g = target(i)
+        b = (i // owners) * owners + owner_of(i)
 
         def piece(f, s):
-            return spread.at[f * (gz_count // 2) + g // 2, g % 2, s]
+            return spread.at[f * (gz_count // 2) + b // 2, b % 2, s]
 
         def send(f, s):
             pltpu.make_async_remote_copy(
-                src_ref=piece(f, s), dst_ref=mix.at[g, slot + s],
-                send_sem=mix_sent, recv_sem=mix_come.at[g],
+                src_ref=piece(f, s), dst_ref=mix.at[b, slot + s],
+                send_sem=mix_sent, recv_sem=mix_come.at[b],
                 device_id=(f, me_gz), device_id_type=MESH,
             ).start()
 
         def keep(s):
             pltpu.make_async_copy(
-                piece(me_field, s), mix.at[g, slot + s], mix_come.at[g]
+                piece(me_field, s), mix.at[b, slot + s], mix_come.at[b]
             ).start()
 
         others = [lax.rem(me_field + 2, 4), me_field + 1 - 2 * (me_field % 2), 3 - me_field]
@@ -781,51 +791,82 @@
 
     loop(0, gz_count, mix_send)
     build_table(length, coarse_ref, fine_ref, table)
+    acc[...] = jnp.zeros_like(acc)
 
     def join_send(i):
-        g = target(i)
-        pltpu.make_async_copy(mix.at[g], mix.at[g], mix_come.at[g]).wait()
-        wave_x = (length // 4 + me_field * (gz_count // 2) + g // 2).astype(jnp.float32)
+        chunk, owner = i // owners, owner_of(i)
+        b = chunk * owners + owner
+        wait(mix.at[b], mix_come.at[b])
+        wave_x = (length // 4 + me_field * (gz_count // 2) + b // 2).astype(jnp.float32)
         lane = lax.broadcasted_iota(jnp.int32, (1, 2 * LANES), 1) % LANES
-        wave_y = (length // 8 + (g % 2) * LANES + lane).astype(jnp.float32)
+        wave_y = (length // 8 + (b % 2) * LANES + lane).astype(jnp.float32)
         weight = 3.0 * wave_x * wave_y
         for parity in range(2):
-            value = mix[g, 5, parity].astype(jnp.float32)
-            value = value + weight * mix[g, 4, parity].astype(jnp.float32)
-            joined[g, parity] = value.astype(jnp.bfloat16)
+            value = mix[b, 5, parity].astype(jnp.float32)
+            value = value + weight * mix[b, 4, parity].astype(jnp.float32)
+            joined[b, parity] = value.astype(jnp.bfloat16)
+        base = (mix.at[b, 0], first.at[chunk, me_plane, 0, :, me_core])
+        me_near = me_plane % 2
         pairs = (
-            (mix.at[g, pl.ds(0, 4)], land.at[me_plane, pl.ds(0, 4), :, me_core]),
-            (joined.at[g], land.at[me_plane, 4, :, me_core]),
-        )
-
-        @pl.when(g != me_gz)
+            (mix.at[b, pl.ds(1, 3)], land.at[chunk, me_near, pl.ds(0, 3), :, me_core]),
+            (joined.at[b], land.at[chunk, me_near, 3, :, me_core]),
+        )
+        forward(*base, land_sent, first_come.at[chunk, me_gz], (1 - me_half) * owners + owner)
+
+        @pl.when(owner != me_owner)
         def _():
+            g = me_half * owners + owner
+            forward(*base, land_sent, first_come.at[chunk, me_gz], g)
             for source, goal in pairs:
-                pltpu.make_async_remote_copy(
-                    src_ref=source, dst_ref=goal,
-                    send_sem=land_sent, recv_sem=land_come.at[me_gz],
-                    device_id=(me_field, g), device_id_type=MESH,
-                ).start()
-
-        @pl.when(g == me_gz)
+                forward(source, goal, land_sent, land_come.at[chunk, me_owner], g)
+
+        @pl.when(owner == me_owner)
         def _():
+            pltpu.make_async_copy(*base, first_come.at[chunk, me_gz]).start()
             for source, goal in pairs:
-                pltpu.make_async_copy(source, goal, land_come.at[me_gz]).start()
-
-    loop(0, gz_count // 2, join_send)
-    pltpu.make_async_copy(index, index, index_come).wait()
-    split_keys(index, keys)
-    loop(gz_count // 2, gz_count, join_send)
-
-    near = 1 - 2 * (me_plane % 2)
-    for j, steps in enumerate((2, near, 0, 2 + near)):
-        plane = lax.rem(me_plane + steps, planes_z)
-        for core in range(cores):
-            block = land.at[plane, :, :, core]
-            pltpu.make_async_copy(block, block, land_come.at[plane * cores + core]).wait()
-        accumulate(table, land, prod, plane, j == 0)
-
-    histogram(length, me_field * gz_count + me_gz, prod, vals, keys, acc)
+                pltpu.make_async_copy(source, goal, land_come.at[chunk, me_owner]).start()
+
+    def transform(chunk):
+        near = 1 - 2 * (me_plane % 2)
+        for n, hop in enumerate((0, near)):
+            plane = me_plane + hop
+            local = plane % 2
+            for core in range(cores):
+                wait(land.at[chunk, local, :, :, core], land_come.at[chunk, local * cores + core])
+            accumulate(table, land.at[chunk], prod, plane, local, KEPT - 1, 1, n == 0)
+        for n in range(planes_z):
+            plane = lax.rem(me_plane + n, planes_z)
+            for core in range(cores):
+                block = first.at[chunk, plane, :, :, core]
+                wait(block, first_come.at[chunk, plane * cores + core])
+            accumulate(table, first.at[chunk], prod, plane, plane, 1, 0, n == 0)
+
+    tiles = length // 32
+    span = tiles // owners
+
+    def bin_lines(chunk, n, count):
+        b = me_field * gz_count + chunk * owners + me_owner
+        histogram(
+            length, b, prod, vals, keys.at[chunk], acc, n * span, (n + count) * span
+        )
+
+    loop(0, owners, join_send)
+    for chunk in range(chunks):
+        wait(index.at[chunk], index_come.at[chunk])
+        split_keys(index.at[chunk], keys.at[chunk])
+    join_send(owners)
+    transform(0)
+
+    def mixed_step(n):
+        bin_lines(0, n, 1)
+
+        @pl.when(n < owners - 1)
+        def _():
+            join_send(owners + 1 + n)
+
+    loop(0, owners, mixed_step)
+    transform(1)
+    bin_lines(1, 0, owners)
 
     ranks = acc.shape[0] // 8
     root = lax.rem(me_gz, fields) == me_field
@@ -858,40 +899,40 @@
     def _():
         parts[me] = acc[pl.ds(pl.multiple_of(me_gz * 8, 8), 8), :]
         rest = parts.at[pl.ds(0, devices - 1)]
-        pltpu.make_async_copy(rest, rest, part_come).wait()
+        wait(rest, part_come)
         answer[me_gz] = lax.fori_loop(
             1, devices, lambda d, total: total + parts[d], parts[0]
         )
         loop(1, devices, lambda step: answer_copy(step).start())
         got = answer.at[pl.ds(0, ranks - 1)]
-        pltpu.make_async_copy(got, got, answer_come).wait()
-        pltpu.make_async_copy(rest, rest, answer_sent).wait()
-        pltpu.make_async_copy(got, got, part_sent).wait()
+        wait(got, answer_come)
+        wait(rest, answer_sent)
+        wait(got, part_sent)
 
     @pl.when(jnp.logical_not(root))
     def _():
-        pltpu.make_async_copy(answer, answer, answer_come).wait()
-        pltpu.make_async_copy(answer, answer, part_sent).wait()
+        wait(answer, answer_come)
+        wait(answer, part_sent)
 
     for hi in range(2):
-        scale = 1.0 / jnp.maximum(answer[6 + hi], 1.0)
+        scale = 1.0 / jnp.maximum(0.5 * answer[6 + hi], 1.0)
         for m in range(3):
-            out_ref[m, :, hi * LANES : (hi + 1) * LANES] = answer[2 * m + hi] * scale
-
-    sent = index_out.at[pl.ds(0, gz_count - 1)]
-    pltpu.make_async_copy(sent, sent, index_sent).wait()
-    sent = mix.at[pl.ds(0, gz_count - 1), pl.ds(0, KEPT)]
-    pltpu.make_async_copy(sent, sent, land_sent).wait()
+            half_scale = 0.5 * scale if m == 0 else scale
+            out_ref[m, :, hi * LANES : (hi + 1) * LANES] = answer[2 * m + hi] * half_scale
+
+    for _ in range(2):
+        sent = index_out.at[pl.ds(0, gz_count - 1)]
+        wait(sent, index_sent)
+    wait(mix.at[:, 0], land_sent)
+    wait(mix.at[pl.ds(0, 2 * (owners - 1)), pl.ds(0, KEPT)], land_sent)
 
     @pl.when(even == 1)
     def _():
-        sent = spread.at[pl.ds(0, 12)]
-        pltpu.make_async_copy(sent, sent, mix_sent).wait()
+        wait(spread.at[pl.ds(0, 12)], mix_sent)
 
     @pl.when(even == 0)
     def _():
-        sent = spread.at[pl.ds(0, 12), :, 0]
-        pltpu.make_async_copy(sent, sent, mix_sent).wait()
+        wait(spread.at[pl.ds(0, 12), :, 0], mix_sent)
 
 
 def whole(fields, shells, mubins, gz_count):
@@ -903,6 +944,8 @@
     wide = 2 * LANES
     dma = pltpu.SemaphoreType.DMA
     low = jnp.bfloat16
+    line_block = (2, depth // 2, wide)
+    pair_block = (2, 2, depth // 2, wide)
     return pl.pallas_call(
         functools.partial(whole_kernel, length),
         out_shape=jax.ShapeDtypeStruct((3, MUBINS, SHELLS), jnp.float32),
@@ -910,22 +953,23 @@
         out_specs=vmem,
         scratch_shapes=[
             pltpu.VMEM((2, 32) + fields.shape[1:], low),
-            pltpu.VMEM((planes, 2, local, 2, depth // 2, wide), low),
-            pltpu.VMEM((gz_count, SLOTS, 2, depth // 2, wide), low),
-            pltpu.VMEM((gz_count, 2, depth // 2, wide), low),
-            pltpu.VMEM((gz_count // 2, KEPT, 2, 2, depth // 2, wide), low),
+            pltpu.VMEM((planes, 2, local) + line_block, low),
+            pltpu.VMEM((gz_count, SLOTS) + line_block, low),
+            pltpu.VMEM((gz_count,) + line_block, low),
+            pltpu.VMEM((2, gz_count // 2, 1) + pair_block, low),
+            pltpu.VMEM((2, gz_count // 4, KEPT - 1) + pair_block, low),
             pltpu.VMEM((KEPT, 2, half, wide), jnp.float32),
             pltpu.VMEM((gz_count // 2, 2, half, depth), low),
             pltpu.VMEM((2, gz_count, depth, LANES), jnp.int32),
             pltpu.VMEM((gz_count, depth, LANES), jnp.int32),
-            pltpu.VMEM((gz_count, depth, LANES), jnp.int32),
-            pltpu.VMEM((2, length, LANES), jnp.float32),
+            pltpu.VMEM((2, gz_count, depth, LANES), jnp.int32),
+            pltpu.VMEM((2, 2, length, LANES), jnp.float32),
             pltpu.VMEM((3, 32, LANES), jnp.float32),
             pltpu.VMEM((4 * LOW, LANES), jnp.float32),
             pltpu.VMEM((4 * gz_count, 8, LANES), jnp.float32),
             pltpu.VMEM((8, 8, LANES), jnp.float32),
-            dma((2,)), dma((2,)), dma, dma, dma, dma((gz_count,)), dma, dma((gz_count,)),
-            dma, dma, dma, dma,
+            dma((2,)), dma((2,)), dma, dma((2,)), dma, dma((gz_count,)), dma,
+            dma((2, gz_count)), dma((2, gz_count // 2)), dma, dma, dma, dma,
         ],
         compiler_params=pltpu.CompilerParams(
             vmem_limit_bytes=60 * 1024 * 1024, collective_id=2, has_side_effects=True

time: 192 us -> 165 us (0.86)
  Pallas kernels: 190 us -> 164 us
    pallas_call x1, Pallas kernels: 190 us -> 164 us  [whole(): pl.pallas_call(functools.partial(whole_kernel, length), out_shape=jax.Sha...]
where the time goes in v3:
time: 165 us
  Pallas kernels  164 us (99%)
    pallas_call x1, Pallas kernels, whole(): pl.pallas_call(functools.partial(whole_kernel, length), out_shape=jax.Sha...  164 us

profile of v3, /device:TPU:0, one launch (start us, length us, event | category | flops | bytes accessed | tf_op | source)
XLA Modules:
  0.0 165.1 jit_solution(11349086580297958530)
XLA Ops:
  0.0 163.8 %shard_map.55 = f32[3,8,256]{2,1,0:T(8,128)} custom-call(f32[2,2,32,1024]{3,2,1,0:T(8,128)} %constant.4.clone.coarse_ref, f32[2,2,16,1024]{3,2,1,0:T(8,128)} %constant.5.clone.fine_ref, bf16[256,2,2,16,256]{4,3,2,1,0:T(8,128)(2,1)} %fields_ref.1, s32[256,16,256]{2,1,0:T(8,128)} %shells_ref.1, s32[256,16,256]{2,1,0:T(8,128)} %mubins_ref.1), custom_call_target="tpu_custom_call" | custom-call | tf_op jit(solution)/shard_map/pallas_call | solution.py:949
  163.8 1.3 copy.7

commit v4 on v3

--- a/solution.py
+++ b/solution.py
@@ -520,19 +520,37 @@
                 put(value.astype(jnp.bfloat16), h, 0, c)
 
 
-def accumulate(table, land, prod, plane, local, fields, start, fresh):
-    def group(n, carry):
-        a, parity = n // 2, n % 2
-        right = land[local, a, parity].reshape(-1, land.shape[-1])
-        part = jnp.dot(table[plane, parity], right, preferred_element_type=jnp.float32)
-        prod[start + a, parity] = part if fresh else prod[start + a, parity] + part
+def transform(table, land, prod, fields, start, sources, sums):
+    wide = prod.shape[3]
+    quads = [sums[4 * n : 4 * n + 4] for n in range(4)]
+
+    def group(a, carry):
+        for parity in range(2):
+            for n, (plane, local) in enumerate(sources):
+                right = land[local, a, parity].reshape(-1, wide)
+                for mxu in range(2):
+                    pltpu.matmul_push_rhs(right, n % 2, mxu)
+                    for i in range(4):
+                        at = (4 * mxu + i) * LANES
+                        pltpu.matmul_acc_lhs(
+                            quads[2 * mxu + parity][i],
+                            table[plane, parity, at : at + LANES, :],
+                            n % 2 if i == 0 else None,
+                        )
+            for mxu in range(2):
+                for i in range(4):
+                    at = (4 * mxu + i) * LANES
+                    prod[start + a, parity, at : at + LANES, :] = pltpu.matmul_pop(
+                        quads[2 * mxu + parity][i]
+                    )
         return carry
 
-    lax.fori_loop(0, 2 * fields, group, 0)
-
-
-def histogram(length, plane, prod, vals, keys, acc, low, high):
+    lax.fori_loop(0, fields, group, 0)
+
+
+def histogram(length, plane, prod, vals, keys, acc, low, high, sums):
     quarter, half = length // 4, length // 2
+    groups, mxus = 4, 2
     lane = lax.broadcasted_iota(jnp.int32, (8, LANES), 1).astype(jnp.float32)
     wave_x = (length // 4 + plane // 2).astype(jnp.float32)
     wave_y = (length // 8 + (plane % 2) * LANES).astype(jnp.float32) + lane
@@ -551,7 +569,7 @@
             length - k - quarter * start,
         )[j]
 
-    def tile(t, edge):
+    def values(t, edge):
         first = t * 8 if edge else pl.multiple_of(t * 8, 8)
         row = lax.broadcasted_iota(jnp.int32, (8, LANES), 0) + first
         special = row == 0
@@ -608,36 +626,34 @@
             vals[0, j * 8 : j * 8 + 8] = auto
             vals[1, j * 8 : j * 8 + 8] = pair
             vals[2, j * 8 : j * 8 + 8] = quad
-        total = acc[...]
-        for start in range(0, 32, PAIRS):
-            left, hot = [], []
-            for r in range(start, start + PAIRS):
-                cell = cell_row(r // 8, first + r % 8)
-                spread = [
-                    jnp.broadcast_to(part, (16, LANES)).astype(jnp.bfloat16)
-                    for part in [vals[i, r : r + 1] for i in range(3)]
-                    + [keys[i, pl.ds(cell, 1), :] for i in range(2)]
-                ]
-                match = spread[3] == iotas[0]
-                left.append(
-                    jnp.concatenate(
-                        [jnp.where(match, spread[i], none) for i in range(3)]
-                        + [jnp.where(match, one, none)],
-                        axis=0,
-                    )
-                )
-                hot.append(
-                    jnp.concatenate(
-                        [jnp.where(spread[4] == it, one, none) for it in iotas], axis=0
-                    )
-                )
-            total = total + lax.dot_general(
-                jnp.concatenate(left, axis=1),
-                jnp.concatenate(hot, axis=1),
-                (((1,), (1,)), ((), ())),
-                preferred_element_type=jnp.float32,
-            )
-        acc[...] = total
+
+    def one_hots(r, cell):
+        spread = [
+            jnp.broadcast_to(part, (16, LANES)).astype(jnp.bfloat16)
+            for part in [vals[i, r : r + 1] for i in range(3)]
+            + [keys[i, pl.ds(cell, 1), :] for i in range(2)]
+        ]
+        match = spread[3] == iotas[0]
+        left = [jnp.where(match, spread[i], none) for i in range(3)]
+        left = jnp.concatenate(left + [jnp.where(match, one, none)], axis=0)
+        hot = [jnp.where(spread[4] == it, one, none) for it in iotas]
+        return left, jnp.concatenate(hot, axis=0)
+
+    def tile(t, edge):
+        values(t, edge)
+        first = t * 8
+        for unit in range(4):
+            mxu, stage = unit % mxus, unit // mxus
+            lefts, hots = [], []
+            for g in range(groups):
+                pair = []
+                for r in range(unit * 8 + g * 2, unit * 8 + g * 2 + 2):
+                    pair.append(one_hots(r, cell_row(r // 8, first + r % 8)))
+                lefts.append(jnp.concatenate([x[0] for x in pair], axis=1))
+                hots.append(jnp.concatenate([x[1] for x in pair], axis=1))
+            pltpu.matmul_push_rhs(jnp.concatenate(lefts, axis=0), stage, mxu, transpose=True)
+            for g in range(groups):
+                pltpu.matmul_acc_lhs(sums[8 * mxu + g], hots[g], stage if g == 0 else None)
 
     @pl.when(low == 0)
     def _():
@@ -648,6 +664,13 @@
         return carry
 
     lax.fori_loop(jnp.maximum(low, 1), high, step, 0)
+    total = None
+    for g in range(groups):
+        block = pltpu.matmul_pop(sums[g]) + pltpu.matmul_pop(sums[8 + g])
+        block = block[:, g // 2 * LANES : (g // 2 + 1) * LANES]
+        block = jnp.transpose(block)[g % 2 * 64 : g % 2 * 64 + 64]
+        total = block if total is None else total + block
+    acc[...] += total
 
 
 def whole_kernel(
@@ -826,62 +849,76 @@
             for source, goal in pairs:
                 pltpu.make_async_copy(source, goal, land_come.at[chunk, me_owner]).start()
 
-    def transform(chunk):
+    def transform_lines(chunk, sums):
         near = 1 - 2 * (me_plane % 2)
-        for n, hop in enumerate((0, near)):
-            plane = me_plane + hop
-            local = plane % 2
+        sources = [(me_plane + hop, lax.rem(me_plane + hop, 2)) for hop in (0, near)]
+        for _, local in sources:
             for core in range(cores):
                 wait(land.at[chunk, local, :, :, core], land_come.at[chunk, local * cores + core])
-            accumulate(table, land.at[chunk], prod, plane, local, KEPT - 1, 1, n == 0)
-        for n in range(planes_z):
-            plane = lax.rem(me_plane + n, planes_z)
+        transform(table, land.at[chunk], prod, KEPT - 1, 1, sources, sums)
+        sources = [(n, n) for n in range(planes_z)]
+        for plane, _ in sources:
             for core in range(cores):
                 block = first.at[chunk, plane, :, :, core]
                 wait(block, first_come.at[chunk, plane * cores + core])
-            accumulate(table, first.at[chunk], prod, plane, plane, 1, 0, n == 0)
+        transform(table, first.at[chunk], prod, 1, 0, sources, sums)
 
     tiles = length // 32
     span = tiles // owners
 
-    def bin_lines(chunk, n, count):
+    def bin_lines(chunk, n, count, sums):
         b = me_field * gz_count + chunk * owners + me_owner
-        histogram(
-            length, b, prod, vals, keys.at[chunk], acc, n * span, (n + count) * span
-        )
+        low, high = n * span, (n + count) * span
+        histogram(length, b, prod, vals, keys.at[chunk], acc, low, high, sums)
 
     loop(0, owners, join_send)
     for chunk in range(chunks):
         wait(index.at[chunk], index_come.at[chunk])
         split_keys(index.at[chunk], keys.at[chunk])
     join_send(owners)
-    transform(0)
-
-    def mixed_step(n):
-        bin_lines(0, n, 1)
-
-        @pl.when(n < owners - 1)
-        def _():
-            join_send(owners + 1 + n)
-
-    loop(0, owners, mixed_step)
-    transform(1)
-    bin_lines(1, 0, owners)
+
+    def crunch(*sums):
+        for ref in sums:
+            pltpu.matmul_pop(ref)
+        transform_lines(0, sums)
+
+        def mixed_step(n):
+            bin_lines(0, n, 1, sums)
+
+            @pl.when(n < owners - 1)
+            def _():
+                join_send(owners + 1 + n)
+
+        loop(0, owners, mixed_step)
+        transform_lines(1, sums)
+        bin_lines(1, 0, owners, sums)
+
+    pl.run_scoped(
+        crunch,
+        *(
+            pltpu.ACC(mxu)((LANES, 2 * LANES), jnp.float32)
+            for mxu in range(2)
+            for _ in range(8)
+        ),
+    )
 
     ranks = acc.shape[0] // 8
-    root = lax.rem(me_gz, fields) == me_field
+    middle = (planes_z // 2 - 1) * cores
+    rank = me_field + fields * lax.div(me_gz - middle, cores)
+    root = (me_gz == middle) | (me_gz == middle + cores)
 
     def part_copy(r):
         return pltpu.make_async_remote_copy(
             src_ref=acc.at[pl.ds(pl.multiple_of(r * 8, 8), 8)], dst_ref=parts.at[me],
             send_sem=part_sent, recv_sem=part_come,
-            device_id=(lax.rem(r, fields), r), device_id_type=MESH,
+            device_id=(lax.rem(r, fields), middle + cores * (r // fields)),
+            device_id_type=MESH,
         )
 
     def part_send(n):
-        r = lax.rem(me_gz + n, ranks)
-
-        @pl.when((r != me_gz) | jnp.logical_not(root))
+        r = lax.rem(me_field + n, ranks)
+
+        @pl.when((r != rank) | jnp.logical_not(root))
         def _():
             part_copy(r).start()
 
@@ -890,17 +927,17 @@
     def answer_copy(step):
         other = lax.rem(me + step, devices)
         return pltpu.make_async_remote_copy(
-            src_ref=answer.at[me_gz], dst_ref=answer.at[me_gz],
+            src_ref=answer.at[rank], dst_ref=answer.at[rank],
             send_sem=answer_sent, recv_sem=answer_come,
             device_id=(other // gz_count, lax.rem(other, gz_count)), device_id_type=MESH,
         )
 
     @pl.when(root)
     def _():
-        parts[me] = acc[pl.ds(pl.multiple_of(me_gz * 8, 8), 8), :]
+        parts[me] = acc[pl.ds(pl.multiple_of(rank * 8, 8), 8), :]
         rest = parts.at[pl.ds(0, devices - 1)]
         wait(rest, part_come)
-        answer[me_gz] = lax.fori_loop(
+        answer[rank] = lax.fori_loop(
             1, devices, lambda d, total: total + parts[d], parts[0]
         )
         loop(1, devices, lambda step: answer_copy(step).start())
@@ -987,9 +1024,9 @@
     width = plane_rows // devices
     me_gz, me_field = lax.axis_index("gz"), lax.axis_index("field")
 
-    if (field_count, gz_count, local_fields, planes, yrows) == (4, 8, 2, 16, 256):
-        if depth_local == 256 and (SHELLS, MUBINS) == (256, 8):
-            return whole(fields, shells, mubins, gz_count)
+    paired = yrows == 2 * LANES and 2 * planes == devices and local_fields == 2
+    if paired and depth_local == 2 * LANES and gz_count == 2 * field_count == MUBINS:
+        return whole(fields, shells, mubins, gz_count)
 
     exchange = width == LANES and depth_local % 32 == 0
     if exchange:

time: 165 us -> 163 us (0.988)
  Pallas kernels: 164 us -> 161 us
    pallas_call x1, Pallas kernels: 164 us -> 161 us  [whole(): pl.pallas_call(functools.partial(whole_kernel, length), out_shape=jax.Sha...]
where the time goes in v4:
time: 163 us; the launch traced here: 162 us
  Pallas kernels  161 us (99%)
    pallas_call x1, Pallas kernels, whole(): pl.pallas_call(functools.partial(whole_kernel, length), out_shape=jax.Sha...  161 us

profile of v4, /device:TPU:0, one launch (start us, length us, event | category | flops | bytes accessed | tf_op | source)
XLA Modules:
  0.0 162.3 jit_solution(2264301056137208901)
XLA Ops:
  0.0 160.9 %shard_map.55 = f32[3,8,256]{2,1,0:T(8,128)} custom-call(f32[2,2,32,1024]{3,2,1,0:T(8,128)} %constant.4.clone.coarse_ref, f32[2,2,16,1024]{3,2,1,0:T(8,128)} %constant.5.clone.fine_ref, bf16[256,2,2,16,256]{4,3,2,1,0:T(8,128)(2,1)} %fields_ref.1, s32[256,16,256]{2,1,0:T(8,128)} %shells_ref.1, s32[256,16,256]{2,1,0:T(8,128)} %mubins_ref.1), custom_call_target="tpu_custom_call" | custom-call | tf_op jit(solution)/shard_map/pallas_call | solution.py:986
  160.9 1.3 copy.7

commit v5 on v4

--- a/solution.py
+++ b/solution.py
@@ -548,7 +548,7 @@
     lax.fori_loop(0, fields, group, 0)
 
 
-def histogram(length, plane, prod, vals, keys, acc, low, high, sums):
+def histogram(length, plane, prod, vals, keys, acc, low, high, sums, counting):
     quarter, half = length // 4, length // 2
     groups, mxus = 4, 2
     lane = lax.broadcasted_iota(jnp.int32, (8, LANES), 1).astype(jnp.float32)
@@ -569,7 +569,7 @@
             length - k - quarter * start,
         )[j]
 
-    def values(t, edge):
+    def values(t, edge, slot):
         first = t * 8 if edge else pl.multiple_of(t * 8, 8)
         row = lax.broadcasted_iota(jnp.int32, (8, LANES), 0) + first
         special = row == 0
@@ -623,24 +623,23 @@
             qre = mixed[j][0] + three * cross_b[j][0] + half_more * cubic[j][0]
             qim = mixed[j][1] + three * cross_b[j][1] + half_more * cubic[j][1]
             quad = inverse[j] * (re * qre + im * qim) - 0.5 * pair
-            vals[0, j * 8 : j * 8 + 8] = auto
-            vals[1, j * 8 : j * 8 + 8] = pair
-            vals[2, j * 8 : j * 8 + 8] = quad
-
-    def one_hots(r, cell):
+            vals[slot, 0, j * 8 : j * 8 + 8] = jnp.where(counting, 1.0, auto)
+            vals[slot, 1, j * 8 : j * 8 + 8] = pair
+            vals[slot, 2, j * 8 : j * 8 + 8] = quad
+
+    def one_hots(r, cell, slot):
         spread = [
             jnp.broadcast_to(part, (16, LANES)).astype(jnp.bfloat16)
-            for part in [vals[i, r : r + 1] for i in range(3)]
+            for part in [vals[slot, i, r : r + 1] for i in range(3)]
             + [keys[i, pl.ds(cell, 1), :] for i in range(2)]
         ]
         match = spread[3] == iotas[0]
         left = [jnp.where(match, spread[i], none) for i in range(3)]
-        left = jnp.concatenate(left + [jnp.where(match, one, none)], axis=0)
+        left = jnp.concatenate(left + [none], axis=0)
         hot = [jnp.where(spread[4] == it, one, none) for it in iotas]
         return left, jnp.concatenate(hot, axis=0)
 
-    def tile(t, edge):
-        values(t, edge)
+    def units(t, slot):
         first = t * 8
         for unit in range(4):
             mxu, stage = unit % mxus, unit // mxus
@@ -648,7 +647,7 @@
             for g in range(groups):
                 pair = []
                 for r in range(unit * 8 + g * 2, unit * 8 + g * 2 + 2):
-                    pair.append(one_hots(r, cell_row(r // 8, first + r % 8)))
+                    pair.append(one_hots(r, cell_row(r // 8, first + r % 8), slot))
                 lefts.append(jnp.concatenate([x[0] for x in pair], axis=1))
                 hots.append(jnp.concatenate([x[1] for x in pair], axis=1))
             pltpu.matmul_push_rhs(jnp.concatenate(lefts, axis=0), stage, mxu, transpose=True)
@@ -657,13 +656,20 @@
 
     @pl.when(low == 0)
     def _():
-        tile(0, True)
-
-    def step(t, carry):
-        tile(t, False)
+        values(0, True, 0)
+
+    @pl.when(low != 0)
+    def _():
+        values(low, False, 0)
+
+    def step(n, carry):
+        for i in range(4):
+            t = low + 4 * n + i
+            units(t, i % 2)
+            values(jnp.minimum(t + 1, quarter // 8 - 1), False, 1 - i % 2)
         return carry
 
-    lax.fori_loop(jnp.maximum(low, 1), high, step, 0)
+    lax.fori_loop(0, (high - low) // 4, step, 0)
     total = None
     for g in range(groups):
         block = pltpu.matmul_pop(sums[g]) + pltpu.matmul_pop(sums[8 + g])
@@ -866,10 +872,9 @@
     tiles = length // 32
     span = tiles // owners
 
-    def bin_lines(chunk, n, count, sums):
+    def bin_lines(chunk, low, high, sums):
         b = me_field * gz_count + chunk * owners + me_owner
-        low, high = n * span, (n + count) * span
-        histogram(length, b, prod, vals, keys.at[chunk], acc, low, high, sums)
+        histogram(length, b, prod, vals, keys.at[chunk], acc, low, high, sums, me_half == 1)
 
     loop(0, owners, join_send)
     for chunk in range(chunks):
@@ -880,18 +885,23 @@
     def crunch(*sums):
         for ref in sums:
             pltpu.matmul_pop(ref)
-        transform_lines(0, sums)
-
-        def mixed_step(n):
-            bin_lines(0, n, 1, sums)
+
+        def part(n):
+            chunk = n // owners
+
+            @pl.when(n % owners == 0)
+            def _():
+                transform_lines(chunk, sums)
+
+            low = lax.rem(n, owners) * span
+            high = low + span + chunk * (tiles - span)
+            bin_lines(chunk, low, high, sums)
 
             @pl.when(n < owners - 1)
             def _():
                 join_send(owners + 1 + n)
 
-        loop(0, owners, mixed_step)
-        transform_lines(1, sums)
-        bin_lines(1, 0, owners, sums)
+        loop(0, owners + 1, part)
 
     pl.run_scoped(
         crunch,
@@ -902,6 +912,9 @@
         ),
     )
 
+    counted = acc[0:LOW, :]
+    acc[0:LOW, :] = jnp.where(me_half == 1, 0.0, counted)
+    acc[3 * LOW : 4 * LOW, :] = jnp.where(me_half == 1, counted, 0.0)
     ranks = acc.shape[0] // 8
     middle = (planes_z // 2 - 1) * cores
     rank = me_field + fields * lax.div(me_gz - middle, cores)
@@ -952,10 +965,9 @@
         wait(answer, part_sent)
 
     for hi in range(2):
-        scale = 1.0 / jnp.maximum(0.5 * answer[6 + hi], 1.0)
+        scale = 1.0 / jnp.maximum(answer[6 + hi], 1.0)
         for m in range(3):
-            half_scale = 0.5 * scale if m == 0 else scale
-            out_ref[m, :, hi * LANES : (hi + 1) * LANES] = answer[2 * m + hi] * half_scale
+            out_ref[m, :, hi * LANES : (hi + 1) * LANES] = answer[2 * m + hi] * scale
 
     for _ in range(2):
         sent = index_out.at[pl.ds(0, gz_count - 1)]
@@ -1001,7 +1013,7 @@
             pltpu.VMEM((gz_count, depth, LANES), jnp.int32),
             pltpu.VMEM((2, gz_count, depth, LANES), jnp.int32),
             pltpu.VMEM((2, 2, length, LANES), jnp.float32),
-            pltpu.VMEM((3, 32, LANES), jnp.float32),
+            pltpu.VMEM((2, 3, 32, LANES), jnp.float32),
             pltpu.VMEM((4 * LOW, LANES), jnp.float32),
             pltpu.VMEM((4 * gz_count, 8, LANES), jnp.float32),
             pltpu.VMEM((8, 8, LANES), jnp.float32),

time: 163 us -> 156 us (0.957)
  Pallas kernels: 161 us -> 155 us
    pallas_call x1, Pallas kernels: 161 us -> 155 us  [whole(): pl.pallas_call(functools.partial(whole_kernel, length), out_shape=jax.Sha...]
where the time goes in v5:
time: 156 us
  Pallas kernels  155 us (99%)
    pallas_call x1, Pallas kernels, whole(): pl.pallas_call(functools.partial(whole_kernel, length), out_shape=jax.Sha...  155 us

profile of v5, /device:TPU:0, one launch (start us, length us, event | category | flops | bytes accessed | tf_op | source)
XLA Modules:
  0.0 156.0 jit_solution(2074484846772379394)
XLA Ops:
  0.0 154.7 %shard_map.55 = f32[3,8,256]{2,1,0:T(8,128)} custom-call(f32[2,2,32,1024]{3,2,1,0:T(8,128)} %constant.4.clone.coarse_ref, f32[2,2,16,1024]{3,2,1,0:T(8,128)} %constant.5.clone.fine_ref, bf16[256,2,2,16,256]{4,3,2,1,0:T(8,128)(2,1)} %fields_ref.1, s32[256,16,256]{2,1,0:T(8,128)} %shells_ref.1, s32[256,16,256]{2,1,0:T(8,128)} %mubins_ref.1), custom_call_target="tpu_custom_call" | custom-call | tf_op jit(solution)/shard_map/pallas_call | solution.py:998
  154.7 1.3 copy.7

commit v6 on v5

--- a/solution.py
+++ b/solution.py
@@ -663,13 +663,13 @@
         values(low, False, 0)
 
     def step(n, carry):
-        for i in range(4):
-            t = low + 4 * n + i
+        for i in range(8):
+            t = low + 8 * n + i
             units(t, i % 2)
             values(jnp.minimum(t + 1, quarter // 8 - 1), False, 1 - i % 2)
         return carry
 
-    lax.fori_loop(0, (high - low) // 4, step, 0)
+    lax.fori_loop(0, (high - low) // 8, step, 0)
     total = None
     for g in range(groups):
         block = pltpu.matmul_pop(sums[g]) + pltpu.matmul_pop(sums[8 + g])

time: 156 us -> 156 us (level)
  no operation moved by 1% of the time
where the time goes in v6:
time: 156 us
  Pallas kernels  154 us (99%)
    pallas_call x1, Pallas kernels, whole(): pl.pallas_call(functools.partial(whole_kernel, length), out_shape=jax.Sha...  154 us

profile of v6, /device:TPU:0, one launch (start us, length us, event | category | flops | bytes accessed | tf_op | source)
XLA Modules:
  0.0 155.6 jit_solution(607818515759691406)
XLA Ops:
  0.0 154.3 %shard_map.55 = f32[3,8,256]{2,1,0:T(8,128)} custom-call(f32[2,2,32,1024]{3,2,1,0:T(8,128)} %constant.4.clone.coarse_ref, f32[2,2,16,1024]{3,2,1,0:T(8,128)} %constant.5.clone.fine_ref, bf16[256,2,2,16,256]{4,3,2,1,0:T(8,128)(2,1)} %fields_ref.1, s32[256,16,256]{2,1,0:T(8,128)} %shells_ref.1, s32[256,16,256]{2,1,0:T(8,128)} %mubins_ref.1), custom_call_target="tpu_custom_call" | custom-call | tf_op jit(solution)/shard_map/pallas_call | solution.py:998
  154.3 1.3 copy.7
